TPU v7x, 32 devices: a whole 2x2x4 slice. The times are simulated.
32 devices in a mesh: seg: 4 (over z), pair: 8 (over y, x, core).
Axes of the slice: x: 2, y: 2, z: 4, core: 2. Of those that a mesh axis runs over, the one named last changes fastest.
Arguments:
- spectra: bfloat16 [4, 2, 2048, 2048], P('seg', None, None, 'pair'), may hold values from -6 to 6
- pair_lists: int32 [32, 2], P('pair'), may hold values from 0 to 15
- pair_counts: int32 [8], P('pair'), may hold values from 1 to 4, as said below
Outputs:
- correlations: float32 [2048, 32, 128], P('seg', 'pair')
Inputs may be any that keep to these rules, and one draw needn't show every extreme that they name: `pair_counts`: some owner uses exactly 4 slots.
All inputs are finite; a program needn't handle non-finite values.
Results may differ from a plain program's by a relative error of at most 0.0003.
Values may be sent and summed in bfloat16 or wider, within the bound.
No kernel may reach another device: no remote copies, remote signals or barrier semaphores. Data moves between devices by JAX's collectives and lax.ppermute only.
A program may use at most 128 MiB of HBM per device.

v0:
```python
import math
import jax
import jax.numpy as jnp
from jax import lax
from jax.sharding import PartitionSpec as P

TILE = 128
LAG = 2048


def stack_weights(linear_re, linear_im, phase_re, phase_im, total_segments):
    weight = (phase_re * phase_re + phase_im * phase_im) / float(total_segments * total_segments)
    return (linear_re * weight, linear_im * weight)


def accumulate(local_spec, group, source_ids, receiver_ids):
    segs_here = local_spec.shape[0]
    band_bins = local_spec.shape[2]
    tiled_spec = local_spec.reshape(segs_here // group, group, 2, band_bins, -1, TILE)

    def one_group(totals, block):
        source_spec = jnp.take(block, source_ids, axis=3).astype(jnp.float32)
        recv_spec = jnp.take(block, receiver_ids, axis=3).astype(jnp.float32)
        cross_re = source_spec[:, 0] * recv_spec[:, 0] + source_spec[:, 1] * recv_spec[:, 1]
        cross_im = source_spec[:, 1] * recv_spec[:, 0] - source_spec[:, 0] * recv_spec[:, 1]
        magnitude = jnp.sqrt(cross_re * cross_re + cross_im * cross_im + 1.0)
        return (
            (
                totals[0] + jnp.sum(cross_re, axis=0),
                totals[1] + jnp.sum(cross_im, axis=0),
                totals[2] + jnp.sum(cross_re / magnitude, axis=0),
                totals[3] + jnp.sum(cross_im / magnitude, axis=0),
            ),
            None,
        )

    zeros = jnp.zeros((band_bins, source_ids.shape[0], TILE), jnp.float32)
    sums, _ = lax.scan(one_group, (zeros, zeros, zeros, zeros), tiled_spec)
    return sums


def body(spectra, pair_lists, pair_counts):
    seg_dev = spectra.shape[0]
    freq_bins = spectra.shape[2]
    n_pair = lax.axis_size("pair")
    n_seg = lax.axis_size("seg")
    seg_index = lax.axis_index("seg")
    most_slots = pair_lists.shape[0]
    total_segments = seg_dev * n_seg
    lists = lax.all_gather(pair_lists, "pair", axis=0, tiled=True)
    source_ids = lists[:, 0]
    receiver_ids = lists[:, 1]
    sub_bins = freq_bins // (n_pair * n_seg)
    bands = lax.all_to_all(spectra, "pair", split_axis=2, concat_axis=3, tiled=True)
    partial_sums = accumulate(bands, seg_dev, source_ids, receiver_ids)
    shares = (
        lax.psum_scatter(partial_sums[0], "seg", scatter_dimension=0, tiled=True),
        lax.psum_scatter(partial_sums[1], "seg", scatter_dimension=0, tiled=True),
        lax.psum_scatter(partial_sums[2], "seg", scatter_dimension=0, tiled=True),
        lax.psum_scatter(partial_sums[3], "seg", scatter_dimension=0, tiled=True),
    )
    block_start = jnp.arange(n_pair, dtype=jnp.int32) * (freq_bins // n_pair) + seg_index * sub_bins
    stack_re, stack_im = stack_weights(shares[0], shares[1], shares[2], shares[3], total_segments)
    stack_re = stack_re.reshape(sub_bins, n_pair, most_slots, TILE)
    stack_im = stack_im.reshape(sub_bins, n_pair, most_slots, TILE)
    owned = (
        lax.all_to_all(stack_re, "pair", split_axis=1, concat_axis=0, tiled=True),
        lax.all_to_all(stack_im, "pair", split_axis=1, concat_axis=0, tiled=True),
    )
    own_bins = sub_bins * n_pair
    row_index = jnp.arange(own_bins, dtype=jnp.int32)
    bin_index = block_start[row_index // sub_bins] + row_index % sub_bins
    owned_re = owned[0].reshape(own_bins, most_slots, TILE)
    owned_im = owned[1].reshape(own_bins, most_slots, TILE)
    live_mask = (jnp.arange(most_slots, dtype=jnp.int32) < pair_counts[0]).astype(jnp.float32)
    owned_re = (owned_re * live_mask[None, :, None]).reshape(own_bins, most_slots * TILE)
    owned_im = (owned_im * live_mask[None, :, None]).reshape(own_bins, most_slots * TILE)
    lag_rows = LAG // n_seg
    lag_offset = jnp.arange(lax.axis_size("seg") * lag_rows, dtype=jnp.int32) - LAG // 2
    product = lag_offset[:, None] * bin_index[None, :] % (2 * freq_bins)
    angles = product.astype(jnp.float32) * jnp.float32(math.pi / freq_bins)
    terms = jnp.dot(
        jnp.cos(angles),
        owned_re,
        precision=lax.Precision.HIGHEST,
        preferred_element_type=jnp.float32,
    )
    terms = terms - jnp.dot(
        jnp.sin(angles),
        owned_im,
        precision=lax.Precision.HIGHEST,
        preferred_element_type=jnp.float32,
    )
    summed = lax.psum_scatter(
        terms * jnp.float32(1.0 / math.sqrt(freq_bins)), "seg", scatter_dimension=0, tiled=True
    )
    return summed.reshape(lag_rows, most_slots, TILE)


def solution(mesh):
    return jax.shard_map(
        body,
        mesh=mesh,
        in_specs=(P("seg", None, None, "pair"), P("pair", None), P("pair")),
        out_specs=P("seg", "pair", None),
        check_vma=False,
    )
```

profile of v0, /device:TPU:0, one launch (start us, length us, event | category | flops | bytes accessed | tf_op | source)
XLA Modules:
  0.0 561.9 jit_solution(8158701286742860428)
XLA Ops:
  6.5 5.8 %copy.27 = bf16[1,2,2048,256]{3,1,0,2:T(2,128)(2,1)} copy(bf16[1,2,2048,256]{3,2,1,0:T(8,128)(2,1)} %param.5) | data formatting | bytes 4194304 | tf_op args[0]
  12.3 5.2 all-to-all-start
  17.6 29.6 %all-gather = s32[8,4,2]{1,2,0:T(2,128)S(1)} all-gather(s32[1,4,2]{1,2,0:T(2,128)S(1)} %bitcast.100), channel_id=1, replica_groups=mesh['seg'=4,'pair'=8] {'pair'}, dimensions={0}, use_global_device_ids=true | all-gather | bytes 288 | tf_op jit(solution)/shard_map/all_gather | solution.py:50
  48.9 4.0 copy.29
  52.9 3.0 copy.30
  55.9 3.1 gather_fusion
  59.0 3.0 gather_fusion.1
  62.0 2.9 fusion.4
  66.1 6.3 %fusion.11 = (f32[256,32,128]{2,0,1:T(8,128)}, f32[256,32,128]{2,0,1:T(8,128)}, f32[256,32,128]{2,0,1:T(8,128)}) fusion(f32[1,2,256,32,128]{4,2,3,1,0:T(8,128)S(1)} %fusion.3, f32[1,2,256,32,128]{4,2,1,3,0:T(8,128)S(1)} %fusion.4), kind=kLoop, calls=%fused_computation.26 | loop fusion | flops 11534336 | bytes 29360128 | tf_op jit(solution)/shard_map/while/body/eval_jaxpr/div | solution.py:31
  72.4 6.4 %fusion.10 = f32[256,32,128]{2,0,1:T(8,128)} fusion(f32[256,32,128]{2,0,1:T(8,128)} %get-tuple-element.22, f32[256,32,128]{2,0,1:T(8,128)} %get-tuple-element.21), kind=kLoop, calls=%fused_computation.25 | loop fusion | flops 5242880 | bytes 12582912 | tf_op jit(solution)/shard_map/while/body/eval_jaxpr/div | solution.py:32
  81.0 74.2 %reduce-scatter.10.cloned.1.call-done = f32[64,32,128]{2,0,1:T(8,128)} async-done(((f32[256,32,128]{2,0,1:T(8,128)}), f32[64,32,128]{2,0,1:T(8,128)}) %reduce-scatter.10.cloned.1.call-update) | async-done | bytes 1048592 | tf_op jit(solution)/shard_map/reduce_scatter | solution.py:60
  155.2 79.7 %reduce-scatter.12.cloned.1.call-done = f32[64,32,128]{2,0,1:T(8,128)} async-done(((f32[256,32,128]{2,0,1:T(8,128)}), f32[64,32,128]{2,0,1:T(8,128)}) %reduce-scatter.12.cloned.1.call-update) | async-done | bytes 1048592 | tf_op jit(solution)/shard_map/reduce_scatter | solution.py:58
  234.9 79.6 %reduce-scatter.6.cloned.1.call-done = f32[64,32,128]{2,0,1:T(8,128)} async-done(((f32[256,32,128]{2,0,1:T(8,128)}), f32[64,32,128]{2,0,1:T(8,128)}) %reduce-scatter.6.cloned.1.call-update) | async-done | bytes 1048592 | tf_op jit(solution)/shard_map/reduce_scatter | solution.py:57
  314.5 79.6 %reduce-scatter.8.cloned.1.call-done = f32[64,32,128]{2,0,1:T(8,128)} async-done(((f32[256,32,128]{2,0,1:T(8,128)}), f32[64,32,128]{2,0,1:T(8,128)}) %reduce-scatter.8.cloned.1.call-update) | async-done | bytes 1048592 | tf_op jit(solution)/shard_map/reduce_scatter | solution.py:59
  394.1 2.6 fusion.23
  396.7 1.6 copy.38
  398.3 3.6 all-to-all-start.2
  405.0 12.4 %all-to-all-done.2 = f32[64,8,4,128]{3,2,0,1:T(4,128)S(1)} async-done(((f32[64,8,4,128]{3,2,0,1:T(4,128)}), f32[64,8,4,128]{3,2,0,1:T(4,128)S(1)}, u32[]{:S(2)}, u32[]{:S(2)}) %all-to-all-start.2) | async-done | bytes 1048608 | tf_op jit(solution)/shard_map/all_to_all | solution.py:68
  417.4 3.6 all-to-all-start.1
  421.2 4.3 compare_select_fusion.1
  426.1 23.5 %fusion.8 = f32[2048,512]{1,0:T(8,128)} fusion(s32[512]{0:T(512)S(1)} %fusion.24, s32[2048]{0:T(1024)S(1)} %iota_add_fusion, f32[64,8,4,128]{3,2,1,0:T(4,128)S(1)} %bitcast.97, f32[512]{0:T(512)S(1)} %broadcast_bitcast_fusion), kind=kOutput, calls=%fused_computation.22 | convolution fusion | flops 6457393152 | bytes 5255168 | tf_op jit(solution)/shard_map/dot_general | solution.py:88
  449.6 25.5 %subtract_multiply_fusion = f32[2048,512]{1,0:T(8,128)} fusion(f32[2048,512]{1,0:T(8,128)} %fusion.8, s32[512]{0:T(512)S(1)} %fusion.24, s32[2048]{0:T(1024)S(1)} %iota_add_fusion, f32[64,8,4,128]{3,2,1,0:T(4,128)S(1)} %bitcast.98, f32[512]{0:T(512)S(1)} %broadcast_bitcast_fusion), kind=kOutput, calls=%fused_computation.21 | convolution fusion | flops 6459490304 | bytes 9449472 | tf_op jit(solution)/shard_map/dot_general | solution.py:82
  475.2 77.7 %reduce-scatter.14.cloned.1.call-done = f32[512,512]{1,0:T(8,128)} async-done(((f32[2048,512]{1,0:T(8,128)}), f32[512,512]{1,0:T(8,128)}) %reduce-scatter.14.cloned.1.call-update) | async-done | bytes 1048592 | tf_op jit(solution)/shard_map/reduce_scatter | solution.py:94
  552.8 2.5 reshape.186
  (30 shorter events, 8.3 us)
Async XLA Ops:
  6.5 11.0 %copy-start.1 = (s32[4,2]{0,1:T(2,128)S(1)}, s32[4,2]{0,1:T(2,128)}, u32[]{:S(2)}) copy-start(s32[4,2]{0,1:T(2,128)} %param.6) | copy-start | bytes 100
  12.3 35.0 %all-to-all-start = ((bf16[1,2,2048,256]{3,1,0,2:T(2,128)(2,1)}), bf16[1,2,2048,256]{3,1,0,2:T(2,128)(2,1)S(1)}, u32[]{:S(2)}, u32[]{:S(2)}) async-start(bf16[1,2,2048,256]{3,1,0,2:T(2,128)(2,1)} %copy.27), calls=%async_computation | async-start | bytes 4194304 | tf_op jit(solution)/shard_map/all_to_all | solution.py:54
  17.5 137.7 %reduce-scatter.10.cloned.1.call-start = ((), (), s32[]{:S(2)}) async-start(), calls=%async_computation.10 | async-start | bytes 5242880 | tf_op jit(solution)/shard_map/reduce_scatter | solution.py:60
  62.0 3.4 copy-start
  78.9 156.0 %reduce-scatter.12.cloned.1.call-start = ((), (), s32[]{:S(2)}) async-start(), calls=%async_computation.11 | async-start | bytes 5242880 | tf_op jit(solution)/shard_map/reduce_scatter | solution.py:58
  79.6 234.8 %reduce-scatter.6.cloned.1.call-start = ((), (), s32[]{:S(2)}) async-start(), calls=%async_computation.8 | async-start | bytes 5242880 | tf_op jit(solution)/shard_map/reduce_scatter | solution.py:57
  80.4 313.7 %reduce-scatter.8.cloned.1.call-start = ((), (), s32[]{:S(2)}) async-start(), calls=%async_computation.9 | async-start | bytes 5242880 | tf_op jit(solution)/shard_map/reduce_scatter | solution.py:59
  398.3 19.1 %all-to-all-start.2 = ((f32[64,8,4,128]{3,2,0,1:T(4,128)}), f32[64,8,4,128]{3,2,0,1:T(4,128)S(1)}, u32[]{:S(2)}, u32[]{:S(2)}) async-start(f32[64,8,4,128]{3,2,0,1:T(4,128)} %copy.38), calls=%async_computation.6 | async-start | bytes 2097152 | tf_op jit(solution)/shard_map/all_to_all | solution.py:68
  417.4 32.3 %all-to-all-start.1 = ((f32[64,8,4,128]{3,2,0,1:T(4,128)}), f32[64,8,4,128]{3,2,0,1:T(4,128)S(1)}, u32[]{:S(2)}, u32[]{:S(2)}) async-start(f32[64,8,4,128]{3,2,0,1:T(4,128)} %copy.37), calls=%async_computation.4 | async-start | bytes 2097152 | tf_op jit(solution)/shard_map/all_to_all | solution.py:67
  420.9 131.9 %reduce-scatter.14.cloned.1.call-start = ((), (), s32[]{:S(2)}) async-start(), calls=%async_computation.12 | async-start | bytes 5242880 | tf_op jit(solution)/shard_map/reduce_scatter | solution.py:94
Sparse Core Ops, SparseCore 0:
  79.0 76.1 reduce-scatter.9
  157.6 77.2 reduce-scatter.11
  237.2 77.2 reduce-scatter.5
  316.7 77.2 reduce-scatter.7
  475.3 77.5 reduce-scatter.13
where the time goes:
time: 563 us; the launch traced here: 562 us
  waiting for transfers between devices  405 us (72%)
  matrix products  49 us (9%)
  blocking collectives  29.6 us (5%)
  local copies, waits for them, and re-layouts  27.6 us (5%)
  other arithmetic  23.9 us (4%)
  between operations  13.9 us (2%)
  starting transfers between devices  12.7 us (2%)
    reduce_scatter x1, waiting for transfers between devices, body(): lax.psum_scatter(partial_sums[1], 'seg', scatter_dimension=0, tiled=True)  79.7 us
    reduce_scatter x1, waiting for transfers between devices, body(): lax.psum_scatter(partial_sums[0], 'seg', scatter_dimension=0, tiled=True)  79.6 us
    reduce_scatter x1, waiting for transfers between devices, body(): lax.psum_scatter(partial_sums[2], 'seg', scatter_dimension=0, tiled=True)  79.6 us
    reduce_scatter x1, waiting for transfers between devices, body(): lax.psum_scatter(terms * jnp.float32(1.0 / math.sqrt(freq_bins)), 'seg',...  77.7 us
    reduce_scatter x1, waiting for transfers between devices, body(): lax.psum_scatter(partial_sums[3], 'seg', scatter_dimension=0, tiled=True)  74.2 us
    all_gather x1, blocking collectives, body(): lists = lax.all_gather(pair_lists, 'pair', axis=0, tiled=True)  29.6 us
    dot_general x1, matrix products, body(): jnp.dot(jnp.cos(angles), owned_re, precision=lax.Precision.HIGHEST, prefe...  25.5 us
    dot_general x1, matrix products, body(): jnp.dot(jnp.sin(angles), owned_im, precision=lax.Precision.HIGHEST, prefe...  23.5 us
  transfers between devices with their start and end apart: 8, of which 6 were waited for; matrix products, arithmetic and copies ran while one was open for 6% of the time, Pallas kernels for 0%

commit v1 on v0

--- a/solution.py
+++ b/solution.py
@@ -3,6 +3,7 @@
 import jax.numpy as jnp
 from jax import lax
 from jax.sharding import PartitionSpec as P
+from jax.lax import all_to_all, axis_size
 
 TILE = 128
 LAG = 2048
@@ -65,7 +66,12 @@
     stack_im = stack_im.reshape(sub_bins, n_pair, most_slots, TILE)
     owned = (
         lax.all_to_all(stack_re, "pair", split_axis=1, concat_axis=0, tiled=True),
-        lax.all_to_all(stack_im, "pair", split_axis=1, concat_axis=0, tiled=True),
+        jnp.concatenate(
+            all_to_all(
+                jnp.stack(jnp.split(stack_im, axis_size("pair"), axis=1), axis=0), "pair", 0, 0
+            ),
+            axis=0,
+        ),
     )
     own_bins = sub_bins * n_pair
     row_index = jnp.arange(own_bins, dtype=jnp.int32)

time: 563 us -> 567 us (level)
  no operation moved by 1% of the time
where the time goes in v1:
time: 567 us; the launch traced here: 566 us
  waiting for transfers between devices  405 us (71%)
  matrix products  49 us (9%)
  local copies, waits for them, and re-layouts  31.9 us (6%)
  blocking collectives  29.6 us (5%)
  other arithmetic  23.9 us (4%)
  between operations  13.9 us (2%)
  starting transfers between devices  12.7 us (2%)
    reduce_scatter x1, waiting for transfers between devices, body(): lax.psum_scatter(partial_sums[1], 'seg', scatter_dimension=0, tiled=True)  79.7 us
    reduce_scatter x1, waiting for transfers between devices, body(): lax.psum_scatter(partial_sums[0], 'seg', scatter_dimension=0, tiled=True)  79.6 us
    reduce_scatter x1, waiting for transfers between devices, body(): lax.psum_scatter(partial_sums[2], 'seg', scatter_dimension=0, tiled=True)  79.6 us
    reduce_scatter x1, waiting for transfers between devices, body(): lax.psum_scatter(terms * jnp.float32(1.0 / math.sqrt(freq_bins)), 'seg',...  77.7 us
    reduce_scatter x1, waiting for transfers between devices, body(): lax.psum_scatter(partial_sums[3], 'seg', scatter_dimension=0, tiled=True)  74.2 us
    all_gather x1, blocking collectives, body(): lists = lax.all_gather(pair_lists, 'pair', axis=0, tiled=True)  29.6 us
    dot_general x1, matrix products, body(): jnp.dot(jnp.cos(angles), owned_re, precision=lax.Precision.HIGHEST, prefe...  25.5 us
    dot_general x1, matrix products, body(): jnp.dot(jnp.sin(angles), owned_im, precision=lax.Precision.HIGHEST, prefe...  23.5 us
  transfers between devices with their start and end apart: 8, of which 6 were waited for; matrix products, arithmetic and copies ran while one was open for 6% of the time, Pallas kernels for 0%

profile of v1, /device:TPU:0, one launch (start us, length us, event | category | flops | bytes accessed | tf_op | source)
XLA Modules:
  0.0 566.3 jit_solution(10512179582923542442)
XLA Ops:
  6.5 5.8 %copy.34 = bf16[1,2,2048,256]{3,1,0,2:T(2,128)(2,1)} copy(bf16[1,2,2048,256]{3,2,1,0:T(8,128)(2,1)} %param.5) | data formatting | bytes 4194304 | tf_op args[0]
  12.3 5.2 all-to-all-start
  17.6 29.6 %all-gather = s32[8,4,2]{1,2,0:T(2,128)S(1)} all-gather(s32[1,4,2]{1,2,0:T(2,128)S(1)} %bitcast.136), channel_id=1, replica_groups=mesh['seg'=4,'pair'=8] {'pair'}, dimensions={0}, use_global_device_ids=true | all-gather | bytes 288 | tf_op jit(solution)/shard_map/all_gather | solution.py:51
  48.9 4.0 copy.36
  52.9 3.0 copy.37
  55.9 3.1 gather_fusion
  59.0 3.0 gather_fusion.1
  62.0 2.9 fusion.4
  66.1 6.3 %fusion.11 = (f32[256,32,128]{2,0,1:T(8,128)}, f32[256,32,128]{2,0,1:T(8,128)}, f32[256,32,128]{2,0,1:T(8,128)}) fusion(f32[1,2,256,32,128]{4,2,3,1,0:T(8,128)S(1)} %fusion.3, f32[1,2,256,32,128]{4,2,1,3,0:T(8,128)S(1)} %fusion.4), kind=kLoop, calls=%fused_computation.26 | loop fusion | flops 11534336 | bytes 29360128 | tf_op jit(solution)/shard_map/while/body/eval_jaxpr/div | solution.py:32
  72.4 6.4 %fusion.10 = f32[256,32,128]{2,0,1:T(8,128)} fusion(f32[256,32,128]{2,0,1:T(8,128)} %get-tuple-element.22, f32[256,32,128]{2,0,1:T(8,128)} %get-tuple-element.21), kind=kLoop, calls=%fused_computation.25 | loop fusion | flops 5242880 | bytes 12582912 | tf_op jit(solution)/shard_map/while/body/eval_jaxpr/div | solution.py:33
  81.0 74.2 %reduce-scatter.10.cloned.1.call-done = f32[64,32,128]{2,0,1:T(8,128)} async-done(((f32[256,32,128]{2,0,1:T(8,128)}), f32[64,32,128]{2,0,1:T(8,128)}) %reduce-scatter.10.cloned.1.call-update) | async-done | bytes 1048592 | tf_op jit(solution)/shard_map/reduce_scatter | solution.py:61
  155.2 79.7 %reduce-scatter.12.cloned.1.call-done = f32[64,32,128]{2,0,1:T(8,128)} async-done(((f32[256,32,128]{2,0,1:T(8,128)}), f32[64,32,128]{2,0,1:T(8,128)}) %reduce-scatter.12.cloned.1.call-update) | async-done | bytes 1048592 | tf_op jit(solution)/shard_map/reduce_scatter | solution.py:59
  234.9 79.6 %reduce-scatter.6.cloned.1.call-done = f32[64,32,128]{2,0,1:T(8,128)} async-done(((f32[256,32,128]{2,0,1:T(8,128)}), f32[64,32,128]{2,0,1:T(8,128)}) %reduce-scatter.6.cloned.1.call-update) | async-done | bytes 1048592 | tf_op jit(solution)/shard_map/reduce_scatter | solution.py:58
  314.5 79.6 %reduce-scatter.8.cloned.1.call-done = f32[64,32,128]{2,0,1:T(8,128)} async-done(((f32[256,32,128]{2,0,1:T(8,128)}), f32[64,32,128]{2,0,1:T(8,128)}) %reduce-scatter.8.cloned.1.call-update) | async-done | bytes 1048592 | tf_op jit(solution)/shard_map/reduce_scatter | solution.py:60
  394.1 2.6 fusion.23
  402.0 3.6 all-to-all-start.2
  407.0 1.6 copy.44
  408.7 12.4 %all-to-all-done.2 = f32[8,64,1,4,128]{4,1,3,2,0:T(8,128)S(1)} async-done(((f32[8,64,1,4,128]{4,1,3,2,0:T(8,128)}), f32[8,64,1,4,128]{4,1,3,2,0:T(8,128)S(1)}, u32[]{:S(2)}, u32[]{:S(2)}) %all-to-all-start.2) | async-done | bytes 1048608 | tf_op jit(solution)/shard_map/all_to_all | solution.py:70
  421.0 3.6 all-to-all-start.1
  424.8 4.3 compare_select_fusion.1
  430.5 23.5 %fusion.8 = f32[2048,512]{1,0:T(8,128)} fusion(s32[512]{0:T(512)S(1)} %fusion.32, s32[2048]{0:T(1024)S(1)} %iota_add_fusion, f32[64,8,4,128]{3,2,1,0:T(4,128)S(1)} %bitcast.134, f32[512]{0:T(512)S(1)} %broadcast_bitcast_fusion), kind=kOutput, calls=%fused_computation.22 | convolution fusion | flops 6457393152 | bytes 5255168 | tf_op jit(solution)/shard_map/dot_general | solution.py:94
  454.0 25.5 %subtract_multiply_fusion = f32[2048,512]{1,0:T(8,128)} fusion(f32[2048,512]{1,0:T(8,128)} %fusion.8, s32[512]{0:T(512)S(1)} %fusion.32, s32[2048]{0:T(1024)S(1)} %iota_add_fusion, f32[64,8,4,128]{3,2,1,0:T(4,128)S(1)} %bitcast.133, f32[512]{0:T(512)S(1)} %broadcast_bitcast_fusion), kind=kOutput, calls=%fused_computation.21 | convolution fusion | flops 6459490304 | bytes 9449472 | tf_op jit(solution)/shard_map/dot_general | solution.py:88
  479.5 77.7 %reduce-scatter.14.cloned.1.call-done = f32[512,512]{1,0:T(8,128)} async-done(((f32[2048,512]{1,0:T(8,128)}), f32[512,512]{1,0:T(8,128)}) %reduce-scatter.14.cloned.1.call-update) | async-done | bytes 1048592 | tf_op jit(solution)/shard_map/reduce_scatter | solution.py:100
  557.2 2.5 reshape.181
  (38 shorter events, 12.6 us)
Async XLA Ops:
  6.5 11.0 %copy-start.1 = (s32[4,2]{0,1:T(2,128)S(1)}, s32[4,2]{0,1:T(2,128)}, u32[]{:S(2)}) copy-start(s32[4,2]{0,1:T(2,128)} %param.6) | copy-start | bytes 100
  12.3 35.0 %all-to-all-start = ((bf16[1,2,2048,256]{3,1,0,2:T(2,128)(2,1)}), bf16[1,2,2048,256]{3,1,0,2:T(2,128)(2,1)S(1)}, u32[]{:S(2)}, u32[]{:S(2)}) async-start(bf16[1,2,2048,256]{3,1,0,2:T(2,128)(2,1)} %copy.34), calls=%async_computation | async-start | bytes 4194304 | tf_op jit(solution)/shard_map/all_to_all | solution.py:55
  17.5 137.7 %reduce-scatter.10.cloned.1.call-start = ((), (), s32[]{:S(2)}) async-start(), calls=%async_computation.10 | async-start | bytes 5242880 | tf_op jit(solution)/shard_map/reduce_scatter | solution.py:61
  62.0 3.4 copy-start
  78.9 156.0 %reduce-scatter.12.cloned.1.call-start = ((), (), s32[]{:S(2)}) async-start(), calls=%async_computation.11 | async-start | bytes 5242880 | tf_op jit(solution)/shard_map/reduce_scatter | solution.py:59
  79.6 234.8 %reduce-scatter.6.cloned.1.call-start = ((), (), s32[]{:S(2)}) async-start(), calls=%async_computation.8 | async-start | bytes 5242880 | tf_op jit(solution)/shard_map/reduce_scatter | solution.py:58
  80.4 313.7 %reduce-scatter.8.cloned.1.call-start = ((), (), s32[]{:S(2)}) async-start(), calls=%async_computation.9 | async-start | bytes 5242880 | tf_op jit(solution)/shard_map/reduce_scatter | solution.py:60
  402.0 19.1 %all-to-all-start.2 = ((f32[8,64,1,4,128]{4,1,3,2,0:T(8,128)}), f32[8,64,1,4,128]{4,1,3,2,0:T(8,128)S(1)}, u32[]{:S(2)}, u32[]{:S(2)}) async-start(f32[8,64,1,4,128]{4,1,3,2,0:T(8,128)} %fusion.24), calls=%async_computation.6 | async-start | bytes 2097152 | tf_op jit(solution)/shard_map/all_to_all | solution.py:70
  421.0 32.9 %all-to-all-start.1 = ((f32[64,8,4,128]{3,2,0,1:T(4,128)}), f32[64,8,4,128]{3,2,0,1:T(4,128)S(1)}, u32[]{:S(2)}, u32[]{:S(2)}) async-start(f32[64,8,4,128]{3,2,0,1:T(4,128)} %copy.44), calls=%async_computation.4 | async-start | bytes 2097152 | tf_op jit(solution)/shard_map/all_to_all | solution.py:68
  424.6 132.6 %reduce-scatter.14.cloned.1.call-start = ((), (), s32[]{:S(2)}) async-start(), calls=%async_computation.12 | async-start | bytes 5242880 | tf_op jit(solution)/shard_map/reduce_scatter | solution.py:100
Sparse Core Ops, SparseCore 0:
  79.0 76.1 reduce-scatter.9
  157.6 77.2 reduce-scatter.11
  237.2 77.2 reduce-scatter.5
  316.7 77.2 reduce-scatter.7
  479.6 77.5 reduce-scatter.13
